TPU v7x, 256 devices: a whole 4x4x8 slice. The times are simulated.
256 devices in a mesh: pair: 32 (over z_hi, x, core), row: 8 (over y, z_lo).
Axes of the slice: x: 4, y: 4, z: 8 (z_hi: 4, z_lo: 2; z = z_hi * 2 + z_lo), core: 2. Of those that a mesh axis runs over, the one named last changes fastest.
Arguments:
- gram_field: float32 [128, 8, 16, 16, 256], P('pair', None, 'row'), may hold values from -3.6 to 3.6, as said below
- left_variance: float32 [128, 16, 16], P('pair'), may hold values from 0.25 to 4
- right_variance: float32 [8, 16, 16], replicated, may hold values from 0.25 to 4
- cotangent: float32 [128, 8, 8, 8, 64], P('pair', 'row'), may hold values from -24 to 24
Outputs:
- gram_gradient: float32 [128, 8, 16, 16, 256], P('pair', None, 'row')
- left_gradient: float32 [128, 16, 16], P('pair')
- right_gradient: float32 [8, 16, 16], replicated
Inputs may be any that keep to these rules, and one draw needn't show every extreme that they name: `gram_field`: each entry lies within 0.9 times the square root of the product of left_variance and right_variance at its two pixels.
All inputs are finite; a program needn't handle non-finite values.
Results may differ from a plain program's by a relative error of at most 0.00008.
Values sent between devices are 32-bit elements; how exact they have to be, the bound alone decides.
No kernel may reach another device: no remote copies, remote signals or barrier semaphores. Data moves between devices by JAX's collectives and lax.ppermute only.
A program may use at most 64 MiB of HBM per device.

v0:
```python
import jax
import jax.numpy as jnp
from jax import lax
from jax.sharding import PartitionSpec as P


def padded_2(block, sides, width):
    for axis, dim in sides:
        count = lax.axis_size(axis)
        forward = [(i, i + 1) for i in range(count - 1)]
        backward = [(target, source) for source, target in forward]
        low = lax.ppermute(
            lax.slice_in_dim(block, block.shape[dim] - width, None, axis=dim), axis, forward
        )
        high = lax.ppermute(lax.slice_in_dim(block, 0, width, axis=dim), axis, backward)
        block = jnp.concatenate([low, block, high], axis=dim)
    return block


def shifted(source, dimension, offset):
    dimension = dimension % source.ndim
    extent = source.shape[dimension]
    margin = abs(offset)
    widths = [(0, 0)] * source.ndim
    widths[dimension] = (margin, margin)
    padded = jnp.pad(source, widths)
    return lax.slice_in_dim(padded, margin + offset, margin + offset + extent, axis=dimension)


def column_masks(length):
    column_index = jnp.arange(length * length) % length
    return (
        (column_index + 1 < length).astype(jnp.float32),
        (column_index >= 1).astype(jnp.float32),
    )


def mix_columns(source, length):
    mask_up, mask_down = column_masks(length)
    return (
        source
        + shifted(shifted(source, -2, 1), -1, 1) * mask_up
        + shifted(shifted(source, -2, -1), -1, -1) * mask_down
    )


def conv_field(padded, length):
    inner = (
        padded[..., 1:-1, :, :]
        + shifted(padded[..., 2:, :, :], -1, length)
        + shifted(padded[..., :-2, :, :], -1, -length)
    )
    return mix_columns(inner, length) / 9.0


def pad_rows(source):
    widths = [(0, 0)] * source.ndim
    widths[source.ndim - 3] = (1, 1)
    return jnp.pad(source, widths)


def conv_map(source):
    row_sum = source + shifted(source, -2, 1) + shifted(source, -2, -1)
    return (row_sum + shifted(row_sum, -1, 1) + shifted(row_sum, -1, -1)) / 9.0


def pool_field(source):
    shape = source.shape
    leading = shape[:-3]
    count = shape[-3]
    length = shape[-2]
    half_side = length // 2
    merged = source.reshape(shape[:-1] + (half_side, 2 * length))
    merged = merged[..., :length] + merged[..., length:]
    merged = merged.reshape(shape[:-1] + (half_side * length,))
    merged = merged[..., 0::2] + merged[..., 1::2]
    merged = merged.reshape(leading + (count // 2, 2, half_side, 2, half_side * half_side))
    return jnp.sum(merged, axis=(-4, -2)) / 16.0


def spread_field(source):
    half_side = source.shape[-2]
    merged = jnp.repeat(source, 2, axis=-3)
    merged = jnp.repeat(merged, 2, axis=-2)
    inner = merged.shape[:-1]
    merged = merged.reshape(inner + (half_side, 1, half_side, 1))
    merged = jnp.broadcast_to(merged, inner + (half_side, 2, half_side, 2))
    return merged.reshape(inner + (4 * half_side * half_side,)) / 16.0


def pool_map(source):
    extent = source.shape[-1] // 2
    merged = source.reshape(source.shape[:-2] + (extent, 2, extent, 2))
    return jnp.mean(merged, axis=(-3, -1))


def spread_map(source):
    return jnp.repeat(jnp.repeat(source, 2, axis=-2), 2, axis=-1) / 4.0


def arc_kernel(source, left, right):
    magnitude = jnp.sqrt(left * right)
    cosine = source / magnitude
    angle_part = jnp.pi - jnp.arccos(cosine)
    sine_part = jnp.sqrt(1.0 - cosine * cosine)
    kernel = magnitude * (sine_part + angle_part * cosine) / (2.0 * jnp.pi)
    slopes = angle_part / (2.0 * jnp.pi)
    weights = magnitude * sine_part / (4.0 * jnp.pi)
    return (kernel, slopes, weights)


def row_window(source, first, count):
    padded = jnp.pad(source, ((0, 0), (2, 2), (0, 0)), constant_values=1.0)
    return lax.dynamic_slice_in_dim(padded, first + 2, count, axis=1)


def on_device(gram_field, left_variance, right_variance, cotangent):
    left_count = gram_field.shape[0]
    shard_rows = gram_field.shape[2]
    length = gram_field.shape[3]
    half_side = length // 2
    count = right_variance.shape[0]
    part_count = cotangent.shape[1]
    rank = lax.axis_index("row")
    zero = rank * 0
    start = rank * shard_rows
    first_left = conv_map(left_variance)
    first_right = conv_map(right_variance)
    right_flat = first_right.reshape(1, count, 1, 1, length * length)
    second_left = conv_map(pool_map(first_left / 2.0))
    second_right = conv_map(pool_map(first_right / 2.0)).reshape(count, half_side * half_side)
    padded = padded_2(gram_field, (("row", 2),), 1)
    source_one = conv_field(padded, length)
    left_rows = row_window(first_left, start, shard_rows)
    kernel_one, slope_one, weight_one = arc_kernel(
        source_one, left_rows[:, None, :, :, None], right_flat
    )
    pooled = pool_field(kernel_one)
    gathered = lax.all_to_all(pooled, "row", split_axis=1, concat_axis=2, tiled=True)
    source_two = conv_field(pad_rows(gathered), half_side)
    first_image = rank * part_count
    second_part = lax.dynamic_slice_in_dim(second_right, first_image, part_count, axis=0)
    unused, slope_two, weight_two = arc_kernel(
        source_two, second_left[:, None, :, :, None], second_part[None, :, None, None, :]
    )
    weighted_two = cotangent * weight_two
    left_two = jnp.sum(weighted_two, axis=(1, 4)) / second_left
    right_part = jnp.sum(weighted_two, axis=(0, 2, 3)) / second_part
    right_two = lax.dynamic_update_slice(
        jnp.zeros((count, half_side * half_side), jnp.float32), right_part, (first_image, zero)
    )
    back_local = conv_field(pad_rows(cotangent * slope_two), half_side)
    back_pooled = lax.all_to_all(back_local, "row", split_axis=2, concat_axis=1, tiled=True)
    back_one = spread_field(back_pooled)
    grad_padded = padded_2(back_one * slope_one, (("row", 2),), 1)
    gram_gradient = conv_field(grad_padded, length)
    weighted_one = back_one * weight_one
    left_local = jnp.sum(weighted_one, axis=(1, 4)) / left_rows
    left_placed = lax.dynamic_update_slice(
        jnp.zeros((left_count, length, length), jnp.float32), left_local, (zero, start, zero)
    )
    left_one = spread_map(conv_map(left_two)) / 2.0 + left_placed
    right_local = jnp.sum(weighted_one, axis=(0, 2, 3)) / first_right.reshape(
        count, length * length
    )
    right_one = spread_map(
        conv_map(right_two.reshape(count, half_side, half_side))
    ) / 2.0 + right_local.reshape(count, length, length)
    left_total = lax.psum(left_one, "row")
    right_total = lax.psum(right_one, ("pair", "row"))
    return (gram_gradient, conv_map(left_total), conv_map(right_total))


def solution(mesh):
    in_specs = (
        P("pair", None, "row", None, None),
        P("pair", None, None),
        P(),
        P("pair", "row", None, None, None),
    )
    out_specs = (P("pair", None, "row", None, None), P("pair", None, None), P())
    return jax.shard_map(
        on_device, mesh=mesh, in_specs=in_specs, out_specs=out_specs, check_vma=False
    )
```

profile of v0, /device:TPU:2, one launch (start us, length us, event | category | flops | bytes accessed | tf_op | source)
XLA Modules:
  0.0 249.3 jit_solution(6002898076283991373)
XLA Ops:
  0.7 2.2 fusion.66
  2.8 3.8 %collective-permute-start.1 = (f32[4,8,1,16,256]{4,3,2,1,0:T(8,128)}, f32[4,8,1,16,256]{4,3,2,1,0:T(8,128)S(1)}, u32[]{:S(2)}, u32[]{:S(2)}) collective-permute-start(f32[4,8,1,16,256]{4,3,2,1,0:T(8,128)} %get-tuple-element.41), channel_id=1, source_target_pairs={{0,1},{1,2},{2,3},{3,4},{4,5},{5,6},{6,7},{8,9},{9,10},{10,11},{11... | collective-permute-start | bytes 1572872 | tf_op jit(solution)/shard_map/ppermute | solution.py:12
  6.7 1.3 collective-permute-start
  9.0 9.2 %collective-permute-done.1 = f32[4,8,1,16,256]{4,3,2,1,0:T(8,128)S(1)} collective-permute-done((f32[4,8,1,16,256]{4,3,2,1,0:T(8,128)}, f32[4,8,1,16,256]{4,3,2,1,0:T(8,128)S(1)}, u32[]{:S(2)}, u32[]{:S(2)}) %collective-permute-start.1) | collective-permute-done | bytes 524320 | tf_op jit(solution)/shard_map/ppermute | solution.py:12
  18.1 12.7 %collective-permute-done = f32[4,8,1,16,256]{4,3,2,1,0:T(8,128)S(1)} collective-permute-done((f32[4,8,1,16,256]{4,3,2,1,0:T(8,128)S(1)}, f32[4,8,1,16,256]{4,3,2,1,0:T(8,128)S(1)}, u32[]{:S(2)}, u32[]{:S(2)}) %collective-permute-start) | collective-permute-done | bytes 524320 | tf_op jit(solution)/shard_map/ppermute | solution.py:15
  30.9 0.8 copy-done.3
  32.5 0.8 copy-done.2
  33.5 4.2 %multiply_multiply_fusion.1 = (f32[4,8,2,16,256]{4,3,2,1,0:T(8,128)}, f32[4,8,2,16,256]{4,3,2,1,0:T(8,128)S(1)}) fusion(f32[8,256]{1,0:T(8,128)S(1)} %copy.153, f32[4,2,16]{2,1,0:T(2,128)S(1)} %pad_dynamic-slice_fusion, f32[256]{0:T(256)S(1)} %get-tuple-element.56, f32[4,8,2,16,256]{4,3,2,1,0:T(8,128)S(1)} %get-tuple-element.39, ...), kind=kLoop, calls=%fused_computation.43 | loop fusion | flops 8650752 | bytes 6302208 | tf_op jit(solution)/shard_map/div | solution.py:106
  37.7 3.7 %reshape.132 = f32[4,8,2,16,8,32]{5,4,3,2,1,0:T(8,128)} reshape(f32[4,8,2,16,256]{4,3,2,1,0:T(8,128)} %get-tuple-element.31) | data formatting | bytes 2097152 | tf_op jit(solution)/shard_map/reshape | solution.py:73
  41.4 6.6 %slice_add_fusion = f32[4,8,2,16,8,16]{5,4,3,2,1,0:T(8,128)} fusion(f32[4,8,2,16,8,32]{5,4,3,2,1,0:T(8,128)} %reshape.132), kind=kLoop, calls=%fused_computation | loop fusion | flops 131072 | bytes 1572864 | tf_op jit(solution)/shard_map/add | solution.py:74
  48.0 3.2 %reshape.133 = f32[4,8,2,16,128]{4,3,2,1,0:T(8,128)S(1)} reshape(f32[4,8,2,16,8,16]{5,4,3,2,1,0:T(8,128)} %slice_add_fusion) | data formatting | bytes 1048576 | tf_op jit(solution)/shard_map/reshape | solution.py:75
  51.3 11.2 %slice.242 = f32[4,8,2,16,64]{4,3,2,1,0:T(8,128)S(1)} slice(f32[4,8,2,16,128]{4,3,2,1,0:T(8,128)S(1)} %reshape.133), slice={[0:4:1], [0:8:1], [0:2:1], [0:16:1], [0:128:2]} | slice | bytes 524288 | tf_op jit(solution)/shard_map/slice | solution.py:76
  62.4 11.3 %slice.243 = f32[4,8,2,16,64]{4,3,2,1,0:T(8,128)S(1)} slice(f32[4,8,2,16,128]{4,3,2,1,0:T(8,128)S(1)} %reshape.133), slice={[0:4:1], [0:8:1], [0:2:1], [0:16:1], [1:128:2]} | slice | bytes 524288 | tf_op jit(solution)/shard_map/slice | solution.py:76
  75.0 5.5 %all-to-all-start = ((f32[8,1,2048]{2,1,0:T(1,128)}), f32[8,1,2048]{2,1,0:T(1,128)S(1)}, u32[]{:S(2)}, u32[]{:S(2)}) async-start(f32[8,1,2048]{2,1,0:T(1,128)} %reshape.138), calls=%async_computation | async-start | bytes 131072 | tf_op jit(solution)/shard_map/all_to_all | solution.py:139
  80.8 6.1 %all-to-all-done = f32[8,1,2048]{2,1,0:T(1,128)S(1)} async-done(((f32[8,1,2048]{2,1,0:T(1,128)}), f32[8,1,2048]{2,1,0:T(1,128)S(1)}, u32[]{:S(2)}, u32[]{:S(2)}) %all-to-all-start) | async-done | bytes 65568 | tf_op jit(solution)/shard_map/all_to_all | solution.py:139
  87.4 0.8 reduce.4
  90.2 3.4 %all-to-all-start.1 = ((f32[8,1,2048]{2,1,0:T(1,128)}), f32[8,1,2048]{2,1,0:T(1,128)S(1)}, u32[]{:S(2)}, u32[]{:S(2)}) async-start(f32[8,1,2048]{2,1,0:T(1,128)} %reshape.140), calls=%async_computation.1 | async-start | bytes 131072 | tf_op jit(solution)/shard_map/all_to_all | solution.py:153
  96.0 3.9 %all-to-all-done.1 = f32[8,1,2048]{2,1,0:T(1,128)S(1)} async-done(((f32[8,1,2048]{2,1,0:T(1,128)}), f32[8,1,2048]{2,1,0:T(1,128)S(1)}, u32[]{:S(2)}, u32[]{:S(2)}) %all-to-all-start.1) | async-done | bytes 65568 | tf_op jit(solution)/shard_map/all_to_all | solution.py:153
  99.8 0.8 reduce.5
  102.1 2.2 copy.171
  104.3 3.5 %broadcast_in_dim.45 = f32[4,8,16,8,2,8,2]{2,1,6,5,4,3,0:T(8,128)} broadcast(f32[4,8,16,8,8]{2,1,4,3,0:T(8,128)} %copy.171), dimensions={0,1,2,3,5} | broadcast | bytes 655360 | tf_op jit(solution)/shard_map/broadcast_in_dim | solution.py:87
  107.8 3.6 %copy.172 = f32[4,8,16,256]{3,2,1,0:T(8,128)} copy(f32[4,8,16,256]{2,1,3,0:T(8,128)} %bitcast.51) | data formatting | bytes 1048576 | tf_op jit(solution)/shard_map/mul | solution.py:157
  112.1 2.2 copy.163
  114.2 3.5 %broadcast_in_dim.19 = f32[4,8,16,8,2,8,2]{2,1,6,5,4,3,0:T(8,128)} broadcast(f32[4,8,16,8,8]{2,1,4,3,0:T(8,128)} %copy.163), dimensions={0,1,2,3,5} | broadcast | bytes 655360 | tf_op jit(solution)/shard_map/broadcast_in_dim | solution.py:87
  117.8 2.8 %copy.164 = f32[4,8,16,256]{3,2,1,0:T(8,128)S(1)} copy(f32[4,8,16,256]{2,1,3,0:T(8,128)} %bitcast.52) | data formatting | bytes 1048576 | tf_op jit(solution)/shard_map/mul | solution.py:155
  120.6 2.7 %fusion.26 = (f32[8,256]{1,0:T(8,128)S(1)}, f32[4,2,16]{2,1,0:T(2,128)S(1)}, f32[4,8,2,16,256]{4,3,2,1,0:T(8,128)S(1)}) fusion(f32[4,8,2,16,256]{4,3,2,1,0:T(8,128)S(1)} %get-tuple-element.32, f32[4,8,16,256]{3,2,1,0:T(8,128)S(1)} %copy-done.5, f32[8,256]{1,0:T(8,128)S(1)} %copy.153, f32[4,2,16]{2,1,0:T(2,128)S(1)} %pad_dynamic-slice_fusion, ...), kind=kLoop, calls=%fused_computation.50 | loop fusion | flops 3143552 | bytes 3163136 | tf_op jit(solution)/shard_map/reduce_sum | solution.py:163
  123.4 0.9 fusion.65
  124.2 2.7 %collective-permute-start.3 = (f32[4,8,1,16,256]{4,3,2,1,0:T(8,128)}, f32[4,8,1,16,256]{4,3,2,1,0:T(8,128)S(1)}, u32[]{:S(2)}, u32[]{:S(2)}) collective-permute-start(f32[4,8,1,16,256]{4,3,2,1,0:T(8,128)} %get-tuple-element.37), channel_id=1, source_target_pairs={{0,1},{1,2},{2,3},{3,4},{4,5},{5,6},{6,7},{8,9},{9,10},{10,11},{11... | collective-permute-start | bytes 1572872 | tf_op jit(solution)/shard_map/ppermute | solution.py:12
  126.9 1.3 collective-permute-start.2
  128.4 81.4 %psum.15 = f32[8,16,16]{0,2,1:T(8,128)S(1)} all-reduce(f32[8,16,16]{0,2,1:T(8,128)S(1)} %divide_add_fusion), channel_id=1, replica_groups=mesh['pair'=32,'row'=8] {'pair','row'}, use_global_device_ids=true, to_apply=%region_9.10 | all-reduce | flops 2048 | bytes 16384 | tf_op jit(solution)/shard_map/psum | solution.py:170
  210.6 34.6 %psum.14 = f32[4,16,16]{2,1,0:T(8,128)S(1)} all-reduce(f32[4,16,16]{2,1,0:T(8,128)S(1)} %add_dynamic-update-slice_fusion), channel_id=1, replica_groups=mesh['pair'=32,'row'=8] {'row'}, use_global_device_ids=true, to_apply=%region_6.7 | all-reduce | flops 1024 | bytes 8192 | tf_op jit(solution)/shard_map/psum | solution.py:169
  247.2 2.1 fusion.9
  (111 shorter events, 13.2 us)
Async XLA Ops:
  0.6 31.0 %copy-start = (f32[4,8,2,16,256]{4,3,2,1,0:T(8,128)S(1)}, f32[4,8,2,16,256]{4,3,2,1,0:T(8,128)}, u32[]{:S(2)}) copy-start(f32[4,8,2,16,256]{4,3,2,1,0:T(8,128)} %param.4) | copy-start | bytes 3145732
  0.6 7.4 %copy-start.12 = (f32[8,16,16]{2,1,0:T(8,128)S(1)}, f32[8,16,16]{2,1,0:T(8,128)}, u32[]{:S(2)}) copy-start(f32[8,16,16]{2,1,0:T(8,128)} %param.6) | copy-start | bytes 24580
  0.7 7.6 %copy-start.13 = (f32[4,16,16]{2,1,0:T(8,128)S(1)}, f32[4,16,16]{2,1,0:T(8,128)}, u32[]{:S(2)}) copy-start(f32[4,16,16]{2,1,0:T(8,128)} %param.5) | copy-start | bytes 12292
  2.8 15.3 %collective-permute-start.1 = (f32[4,8,1,16,256]{4,3,2,1,0:T(8,128)}, f32[4,8,1,16,256]{4,3,2,1,0:T(8,128)S(1)}, u32[]{:S(2)}, u32[]{:S(2)}) collective-permute-start(f32[4,8,1,16,256]{4,3,2,1,0:T(8,128)} %get-tuple-element.41), channel_id=1, source_target_pairs={{0,1},{1,2},{2,3},{3,4},{4,5},{5,6},{6,7},{8,9},{9,10},{10,11},{11... | collective-permute-start | bytes 1572872 | tf_op jit(solution)/shard_map/ppermute | solution.py:12
  6.7 24.2 %collective-permute-start = (f32[4,8,1,16,256]{4,3,2,1,0:T(8,128)S(1)}, f32[4,8,1,16,256]{4,3,2,1,0:T(8,128)S(1)}, u32[]{:S(2)}, u32[]{:S(2)}) collective-permute-start(f32[4,8,1,16,256]{4,3,2,1,0:T(8,128)S(1)} %get-tuple-element.40), channel_id=1, source_target_pairs={{1,0},{2,1},{3,2},{4,3},{5,4},{6,5},{7,6},{9,8},{10,9},{11,10},{12... | collective-permute-start | bytes 1572872 | tf_op jit(solution)/shard_map/ppermute | solution.py:15
  8.4 24.1 %copy-start.9 = (f32[4,16,16]{2,1,0:T(8,128)}, f32[4,16,16]{2,1,0:T(8,128)S(1)}, u32[]{:S(2)}) copy-start(f32[4,16,16]{2,1,0:T(8,128)S(1)} %get-tuple-element.53) | copy-start | bytes 12292
  8.9 23.6 %copy-start.14 = (f32[256]{0:T(256)}, f32[256]{0:T(256)S(1)}, u32[]{:S(2)}) copy-start(f32[256]{0:T(256)S(1)} %get-tuple-element.57) | copy-start | bytes 3076
  18.1 12.7 %copy-start.1 = (f32[4,8,1,16,256]{4,3,2,1,0:T(8,128)}, f32[4,8,1,16,256]{4,3,2,1,0:T(8,128)S(1)}, u32[]{:S(2)}) copy-start(f32[4,8,1,16,256]{4,3,2,1,0:T(8,128)S(1)} %collective-permute-done.1) | copy-start | bytes 1572868
  30.9 0.8 copy-start.3
  32.3 1.0 copy-start.2
  32.3 1.2 copy-start.4
  73.8 14.7 %copy-start.7 = (f32[4,1,8,8,64]{4,3,2,1,0:T(8,128)S(1)}, f32[4,1,8,8,64]{4,3,2,1,0:T(8,128)}, u32[]{:S(2)}) copy-start(f32[4,1,8,8,64]{4,3,2,1,0:T(8,128)} %param.7) | copy-start | bytes 196612
  75.0 11.9 %all-to-all-start = ((f32[8,1,2048]{2,1,0:T(1,128)}), f32[8,1,2048]{2,1,0:T(1,128)S(1)}, u32[]{:S(2)}, u32[]{:S(2)}) async-start(f32[8,1,2048]{2,1,0:T(1,128)} %reshape.138), calls=%async_computation | async-start | bytes 131072 | tf_op jit(solution)/shard_map/all_to_all | solution.py:139
  90.2 9.6 %all-to-all-start.1 = ((f32[8,1,2048]{2,1,0:T(1,128)}), f32[8,1,2048]{2,1,0:T(1,128)S(1)}, u32[]{:S(2)}, u32[]{:S(2)}) async-start(f32[8,1,2048]{2,1,0:T(1,128)} %reshape.140), calls=%async_computation.1 | async-start | bytes 131072 | tf_op jit(solution)/shard_map/all_to_all | solution.py:153
  107.8 3.6 %copy-start.6 = (f32[4,8,8,64]{3,2,0,1:T(8,128)S(1)}, f32[4,8,8,64]{3,2,0,1:T(8,128)}, u32[]{:S(2)}) copy-start(f32[4,8,8,64]{3,2,0,1:T(8,128)} %get-tuple-element.43) | copy-start | bytes 196612
  117.8 2.9 %copy-start.5 = (f32[4,8,16,256]{3,2,1,0:T(8,128)S(1)}, f32[4,8,16,256]{3,2,1,0:T(8,128)}, u32[]{:S(2)}) copy-start(f32[4,8,16,256]{3,2,1,0:T(8,128)} %copy.172) | copy-start | bytes 1572868
  120.6 7.7 %copy-start.8 = (f32[8,16,16]{0,2,1:T(8,128)S(1)}, f32[8,16,16]{0,2,1:T(8,128)}, u32[]{:S(2)}) copy-start(f32[8,16,16]{0,2,1:T(8,128)} %copy.177) | copy-start | bytes 24580
  123.3 86.5 %copy-start.10 = (f32[4,16,16]{2,1,0:T(8,128)S(1)}, f32[4,16,16]{2,1,0:T(8,128)}, u32[]{:S(2)}) copy-start(f32[4,16,16]{2,1,0:T(8,128)} %copy-done.9) | copy-start | bytes 12292
  123.3 86.5 %copy-start.11 = (f32[4,16,16]{2,1,0:T(8,128)S(1)}, f32[4,16,16]{2,1,0:T(8,128)}, u32[]{:S(2)}) copy-start(f32[4,16,16]{2,1,0:T(8,128)} %copy.173) | copy-start | bytes 12292
  124.2 121.7 %collective-permute-start.3 = (f32[4,8,1,16,256]{4,3,2,1,0:T(8,128)}, f32[4,8,1,16,256]{4,3,2,1,0:T(8,128)S(1)}, u32[]{:S(2)}, u32[]{:S(2)}) collective-permute-start(f32[4,8,1,16,256]{4,3,2,1,0:T(8,128)} %get-tuple-element.37), channel_id=1, source_target_pairs={{0,1},{1,2},{2,3},{3,4},{4,5},{5,6},{6,7},{8,9},{9,10},{10,11},{11... | collective-permute-start | bytes 1572872 | tf_op jit(solution)/shard_map/ppermute | solution.py:12
  126.9 119.1 %collective-permute-start.2 = (f32[4,8,1,16,256]{4,3,2,1,0:T(8,128)S(1)}, f32[4,8,1,16,256]{4,3,2,1,0:T(8,128)S(1)}, u32[]{:S(2)}, u32[]{:S(2)}) collective-permute-start(f32[4,8,1,16,256]{4,3,2,1,0:T(8,128)S(1)} %get-tuple-element.36), channel_id=1, source_target_pairs={{1,0},{2,1},{3,2},{4,3},{5,4},{6,5},{7,6},{9,8},{10,9},{11,10},{12... | collective-permute-start | bytes 1572872 | tf_op jit(solution)/shard_map/ppermute | solution.py:15
  246.6 0.6 copy-start.15
where the time goes:
time: 250 us; the launch traced here: 249 us
  blocking collectives  116 us (46%)
  local copies, waits for them, and re-layouts  60.2 us (24%)
  waiting for transfers between devices  31.8 us (13%)
  other arithmetic  22 us (9%)
  starting transfers between devices  18 us (7%)
    psum x1, blocking collectives, on_device(): right_total = lax.psum(right_one, ('pair', 'row'))  81.4 us
    psum x1, blocking collectives, on_device(): left_total = lax.psum(left_one, 'row')  34.6 us
    slice x2, local copies, waits for them, and re-layouts, pool_field(): merged = merged[..., 0::2] + merged[..., 1::2]  22.5 us
    ppermute x2, waiting for transfers between devices, padded_2(): lax.ppermute(lax.slice_in_dim(block, 0, width, axis=dim), axis, backward)  12.7 us
    ppermute x2, waiting for transfers between devices, padded_2(): lax.ppermute(lax.slice_in_dim(block, block.shape[dim] - width, None, axis...  9.17 us
    broadcast_in_dim x2, local copies, waits for them, and re-layouts, spread_field(): merged = jnp.broadcast_to(merged, inner + (half_side, 2, half_side, 2))  7.05 us
    add x1, other arithmetic, pool_field(): merged = merged[..., :length] + merged[..., length:]  6.58 us
    ppermute x2, starting transfers between devices, padded_2(): lax.ppermute(lax.slice_in_dim(block, block.shape[dim] - width, None, axis...  6.51 us
  transfers between devices with their start and end apart: 6, of which 4 were waited for; matrix products, arithmetic and copies ran while one was open for 2% of the time, Pallas kernels for 0%

commit v1 on v0

--- a/solution.py
+++ b/solution.py
@@ -167,7 +167,7 @@
         conv_map(right_two.reshape(count, half_side, half_side))
     ) / 2.0 + right_local.reshape(count, length, length)
     left_total = lax.psum(left_one, "row")
-    right_total = lax.psum(right_one, ("pair", "row"))
+    right_total = jnp.sum(lax.all_gather(right_one, ("pair", "row")), axis=0)
     return (gram_gradient, conv_map(left_total), conv_map(right_total))
 
 

time: 250 us -> 882 us (3.53)
  waiting for transfers between devices: 31.8 us -> 708 us
  blocking collectives: 116 us -> 44.5 us
  between operations: 1.29 us -> 14.7 us
  other arithmetic: 22 us -> 32.3 us
    all_gather x0 -> x1, waiting for transfers between devices: none -> 676 us  [on_device(): right_total = jnp.sum(lax.all_gather(right_one, ('pair', 'row')), axis=0)]
    psum x1 -> x0, blocking collectives: 81.4 us -> none  [on_device(): right_total = lax.psum(right_one, ('pair', 'row'))]
    psum x1, blocking collectives: 34.6 us -> 44.5 us  [on_device(): left_total = lax.psum(left_one, 'row')]
  transfers between devices with their start and end apart: 6 -> 7, of which waited for: 4 -> 5; matrix products, arithmetic and copies ran while one was open for 2% -> 1% of each run, Pallas kernels for 0% -> 0%
where the time goes in v1:
time: 882 us; the launch traced here: 875 us
  waiting for transfers between devices  708 us (80%)
  local copies, waits for them, and re-layouts  57.3 us (6%)
  blocking collectives  44.5 us (5%)
  other arithmetic  32.3 us (4%)
  starting transfers between devices  18 us (2%)
  between operations  14.7 us (2%)
    all_gather x1, waiting for transfers between devices, on_device(): right_total = jnp.sum(lax.all_gather(right_one, ('pair', 'row')), axis=0)  676 us
    psum x1, blocking collectives, on_device(): left_total = lax.psum(left_one, 'row')  44.5 us
    slice x2, local copies, waits for them, and re-layouts, pool_field(): merged = merged[..., 0::2] + merged[..., 1::2]  22.5 us
  transfers between devices with their start and end apart: 7, of which 5 were waited for; matrix products, arithmetic and copies ran while one was open for 1% of the time, Pallas kernels for 0%

profile of v1, /device:TPU:2, one launch (start us, length us, event | category | flops | bytes accessed | tf_op | source)
XLA Modules:
  0.0 874.7 jit_solution(13160356678004263511)
XLA Ops:
  7.2 1.4 fusion.60
  8.6 3.9 collective-permute-start.1
  12.5 1.3 collective-permute-start
  16.0 7.6 collective-permute-done.1
  23.6 12.8 %collective-permute-done = f32[4,8,1,16,256]{4,3,2,1,0:T(8,128)S(1)} collective-permute-done((f32[4,8,1,16,256]{4,3,2,1,0:T(8,128)S(1)}, f32[4,8,1,16,256]{4,3,2,1,0:T(8,128)S(1)}, u32[]{:S(2)}, u32[]{:S(2)}) %collective-permute-start) | collective-permute-done | bytes 524320 | tf_op jit(solution)/shard_map/ppermute | solution.py:15
  38.1 0.8 copy-done.2
  39.0 4.2 multiply_multiply_fusion.1
  43.2 3.7 reshape.132
  47.0 6.6 slice_add_fusion
  53.6 3.2 reshape.133
  56.8 11.2 %slice.242 = f32[4,8,2,16,64]{4,3,2,1,0:T(8,128)S(1)} slice(f32[4,8,2,16,128]{4,3,2,1,0:T(8,128)S(1)} %reshape.133), slice={[0:4:1], [0:8:1], [0:2:1], [0:16:1], [0:128:2]} | slice | bytes 524288 | tf_op jit(solution)/shard_map/slice | solution.py:76
  68.0 11.3 %slice.243 = f32[4,8,2,16,64]{4,3,2,1,0:T(8,128)S(1)} slice(f32[4,8,2,16,128]{4,3,2,1,0:T(8,128)S(1)} %reshape.133), slice={[0:4:1], [0:8:1], [0:2:1], [0:16:1], [1:128:2]} | slice | bytes 524288 | tf_op jit(solution)/shard_map/slice | solution.py:76
  80.6 5.5 all-to-all-start
  86.4 6.1 all-to-all-done
  93.0 0.8 reduce.4
  94.1 0.9 fusion.55
  96.4 3.4 all-to-all-start.1
  101.1 4.9 all-to-all-done.1
  106.0 0.8 reduce.5
  108.3 2.2 copy.154
  110.5 3.5 broadcast_in_dim.45
  114.0 3.5 copy.155
  118.2 2.2 copy.146
  120.4 3.5 broadcast_in_dim.19
  123.9 2.8 copy.147
  126.8 2.7 fusion.26
  130.9 2.7 collective-permute-start.3
  133.6 1.3 collective-permute-start.2
  134.9 44.5 %psum.7 = f32[4,16,16]{2,1,0:T(8,128)S(1)} all-reduce(f32[4,16,16]{2,1,0:T(8,128)S(1)} %add_dynamic-update-slice_fusion), channel_id=1, replica_groups=mesh['pair'=32,'row'=8] {'row'}, use_global_device_ids=true, to_apply=%region_6.7 | all-reduce | flops 1024 | bytes 8192 | tf_op jit(solution)/shard_map/psum | solution.py:169
  181.4 2.1 fusion.9
  183.5 676.4 %all-gather.3.cloned.1.call-done = f32[2048,16,16]{2,1,0:T(8,128)} async-done(((f32[8,16,16]{2,1,0:T(8,128)}), f32[2048,16,16]{2,1,0:T(8,128)}) %all-gather.3.cloned.1.call-update) | async-done | bytes 2097168 | tf_op jit(solution)/shard_map/all_gather | solution.py:170
  860.0 7.1 reduce_sum.94
  (113 shorter events, 15.0 us)
Async XLA Ops:
  7.2 30.0 %copy-start = (f32[4,8,2,16,256]{4,3,2,1,0:T(8,128)S(1)}, f32[4,8,2,16,256]{4,3,2,1,0:T(8,128)}, u32[]{:S(2)}) copy-start(f32[4,8,2,16,256]{4,3,2,1,0:T(8,128)} %param.4) | copy-start | bytes 3145732
  7.2 6.6 copy-start.12
  7.2 6.8 copy-start.13
  8.6 15.0 %collective-permute-start.1 = (f32[4,8,1,16,256]{4,3,2,1,0:T(8,128)S(1)}, f32[4,8,1,16,256]{4,3,2,1,0:T(8,128)S(1)}, u32[]{:S(2)}, u32[]{:S(2)}) collective-permute-start(f32[4,8,1,16,256]{4,3,2,1,0:T(8,128)S(1)} %get-tuple-element.26), channel_id=1, source_target_pairs={{0,1},{1,2},{2,3},{3,4},{4,5},{5,6},{6,7},{8,9},{9,10},{10,11},{11... | collective-permute-start | bytes 1572872 | tf_op jit(solution)/shard_map/ppermute | solution.py:12
  12.5 23.9 %collective-permute-start = (f32[4,8,1,16,256]{4,3,2,1,0:T(8,128)S(1)}, f32[4,8,1,16,256]{4,3,2,1,0:T(8,128)S(1)}, u32[]{:S(2)}, u32[]{:S(2)}) collective-permute-start(f32[4,8,1,16,256]{4,3,2,1,0:T(8,128)S(1)} %get-tuple-element.25), channel_id=1, source_target_pairs={{1,0},{2,1},{3,2},{4,3},{5,4},{6,5},{7,6},{9,8},{10,9},{11,10},{12... | collective-permute-start | bytes 1572872 | tf_op jit(solution)/shard_map/ppermute | solution.py:15
  15.4 22.7 %copy-start.14 = (f32[256]{0:T(256)}, f32[256]{0:T(256)S(1)}, u32[]{:S(2)}) copy-start(f32[256]{0:T(256)S(1)} %get-tuple-element.42) | copy-start | bytes 3076
  23.6 12.8 %copy-start.1 = (f32[4,8,1,16,256]{4,3,2,1,0:T(8,128)}, f32[4,8,1,16,256]{4,3,2,1,0:T(8,128)S(1)}, u32[]{:S(2)}) copy-start(f32[4,8,1,16,256]{4,3,2,1,0:T(8,128)S(1)} %collective-permute-done.1) | copy-start | bytes 1572868
  36.4 0.8 copy-start.3
  37.8 1.0 copy-start.2
  37.8 1.2 copy-start.4
  56.8 29.3 %copy-start.9 = (f32[8,64]{0,1:T(8,128)S(1)}, f32[8,64]{0,1:T(8,128)}, u32[]{:S(2)}) copy-start(f32[8,64]{0,1:T(8,128)} %fusion.49) | copy-start | bytes 6148
  56.8 29.4 %copy-start.10 = (f32[4,8,8]{0,2,1:T(8,128)S(1)}, f32[4,8,8]{0,2,1:T(8,128)}, u32[]{:S(2)}) copy-start(f32[4,8,8]{0,2,1:T(8,128)} %fusion.45) | copy-start | bytes 3076
  79.3 14.7 %copy-start.7 = (f32[4,1,8,8,64]{4,3,2,1,0:T(8,128)S(1)}, f32[4,1,8,8,64]{4,3,2,1,0:T(8,128)}, u32[]{:S(2)}) copy-start(f32[4,1,8,8,64]{4,3,2,1,0:T(8,128)} %param.7) | copy-start | bytes 196612
  80.6 11.9 %all-to-all-start = ((f32[8,1,2048]{2,1,0:T(1,128)}), f32[8,1,2048]{2,1,0:T(1,128)S(1)}, u32[]{:S(2)}, u32[]{:S(2)}) async-start(f32[8,1,2048]{2,1,0:T(1,128)} %reshape.139), calls=%async_computation | async-start | bytes 131072 | tf_op jit(solution)/shard_map/all_to_all | solution.py:139
  96.4 9.6 %all-to-all-start.1 = ((f32[8,1,2048]{2,1,0:T(1,128)}), f32[8,1,2048]{2,1,0:T(1,128)S(1)}, u32[]{:S(2)}, u32[]{:S(2)}) async-start(f32[8,1,2048]{2,1,0:T(1,128)} %reshape.141), calls=%async_computation.1 | async-start | bytes 131072 | tf_op jit(solution)/shard_map/all_to_all | solution.py:153
  99.8 760.2 %all-gather.3.cloned.1.call-start = ((), (), s32[]{:S(2)}) async-start(), calls=%async_computation.2 | async-start | bytes 16842752 | tf_op jit(solution)/shard_map/all_gather | solution.py:170
  114.0 3.6 copy-start.6
  123.9 2.9 copy-start.5
  126.8 2.8 copy-start.8
  126.8 3.5 copy-start.11
  130.9 49.3 %collective-permute-start.3 = (f32[4,8,1,16,256]{4,3,2,1,0:T(8,128)S(1)}, f32[4,8,1,16,256]{4,3,2,1,0:T(8,128)S(1)}, u32[]{:S(2)}, u32[]{:S(2)}) collective-permute-start(f32[4,8,1,16,256]{4,3,2,1,0:T(8,128)S(1)} %get-tuple-element.22), channel_id=1, source_target_pairs={{0,1},{1,2},{2,3},{3,4},{4,5},{5,6},{6,7},{8,9},{9,10},{10,11},{11... | collective-permute-start | bytes 1572872 | tf_op jit(solution)/shard_map/ppermute | solution.py:12
  133.6 46.6 %collective-permute-start.2 = (f32[4,8,1,16,256]{4,3,2,1,0:T(8,128)S(1)}, f32[4,8,1,16,256]{4,3,2,1,0:T(8,128)S(1)}, u32[]{:S(2)}, u32[]{:S(2)}) collective-permute-start(f32[4,8,1,16,256]{4,3,2,1,0:T(8,128)S(1)} %get-tuple-element.21), channel_id=1, source_target_pairs={{1,0},{2,1},{3,2},{4,3},{5,4},{6,5},{7,6},{9,8},{10,9},{11,10},{12... | collective-permute-start | bytes 1572872 | tf_op jit(solution)/shard_map/ppermute | solution.py:15
  180.7 0.7 copy-start.15
Sparse Core Ops, SparseCore 0:
  130.4 729.5 all-gather.2
